TPU v7x, 128 devices: a whole 4x4x4 slice. The times are simulated.
128 devices in a mesh: row: 16 (over y, z), col: 8 (over x, core).
Axes of the slice: x: 4, y: 4, z: 4, core: 2. Of those that a mesh axis runs over, the one named last changes fastest.
Arguments:
- blocks: bfloat16 [16, 8, 128, 4096], P('row', 'col'), may hold values from -0.25 to 0.25
- block_row: int32 [16, 8, 128], P('row', 'col'), may hold values from 0 to 15
- block_col: int32 [16, 8, 128], P('row', 'col'), may hold values from 0 to 31
- counts: int32 [16, 8], P('row', 'col'), may hold values from 0 to 128, as said below
- vectors: float32 [256, 4096], P(('col', 'row')), may hold values from -6 to 6
- row_mass: float32 [256, 64], P(('row', 'col')), may hold values from 0.25 to 4
- col_mass: float32 [256, 64], P(('col', 'row')), may hold values from 0.25 to 4
Outputs:
- subspace: float32 [256, 4096], P(('col', 'row'))
Inputs may be any that keep to these rules, and one draw needn't show every extreme that they name: `counts`: in every row panel one tile uses all 128 slots; every other tile uses at most 8.
All inputs are finite; a program needn't handle non-finite values.
Results may differ from a plain program's by a relative error of at most 0.0085.
Values may be sent and summed in bfloat16 or wider, within the bound.
A program may use at most 64 MiB of HBM per device.

v0:
```python
import functools

import jax
import jax.numpy as jnp
from jax import lax
from jax.experimental import pallas as pl
from jax.experimental.pallas import tpu as pltpu
from jax.sharding import PartitionSpec as P

ITERS = 4
LANES = 512
MESH_ID = pl.DeviceIdType.MESH


def _peer(axis, other, p):
    them = lax.axis_index(other)
    return (p, them) if axis == "row" else (them, p)


def _reduce_kernel(axis, other, n, ch, two_phase, x_ref, o_ref, recv, mine, gath, s1, r1, s2, r2):
    me = lax.axis_index(axis)
    barrier = pltpu.get_barrier_semaphore()
    for d in range(1, n):
        pl.semaphore_signal(
            barrier, 1, device_id=_peer(axis, other, (me + d) % n), device_id_type=MESH_ID
        )
    pl.semaphore_wait(barrier, n - 1)
    if not two_phase:
        sends = []
        for d in range(1, n):
            c = pltpu.make_async_remote_copy(
                x_ref, recv.at[d], s1.at[d], r1.at[d],
                device_id=_peer(axis, other, (me + d) % n), device_id_type=MESH_ID,
            )
            c.start()
            sends.append(c)
        for c in sends:
            c.wait()
        recv[0] = x_ref[...]
        acc = recv[me % n]
        for p in range(1, n):
            acc = acc + recv[(me - p + n) % n]
        o_ref[...] = acc
        return
    sends = []
    for d in range(1, n):
        peer = (me + d) % n
        start = pl.multiple_of(peer * ch, ch)
        c = pltpu.make_async_remote_copy(
            x_ref.at[pl.ds(start, ch)], recv.at[d], s1.at[d], r1.at[d],
            device_id=_peer(axis, other, peer), device_id_type=MESH_ID,
        )
        c.start()
        sends.append(c)
    own = pl.multiple_of(me * ch, ch)
    acc = x_ref[pl.ds(own, ch), :]
    for d, c in enumerate(sends, 1):
        c.wait()
        acc = acc + recv[d]
    mine[...] = acc
    gathers = []
    for d in range(1, n):
        c = pltpu.make_async_remote_copy(
            mine, gath.at[d], s2.at[d], r2.at[d],
            device_id=_peer(axis, other, (me + d) % n), device_id_type=MESH_ID,
        )
        c.start()
        gathers.append(c)
    o_ref[pl.ds(own, ch), :] = acc
    for d, c in enumerate(gathers, 1):
        c.wait()
        src = pl.multiple_of(((me - d + n) % n) * ch, ch)
        o_ref[pl.ds(src, ch), :] = gath[d]


def _gather_kernel(axis, other, n, x_ref, o_ref, gath, s2, r2):
    me = lax.axis_index(axis)
    ch = x_ref.shape[0]
    barrier = pltpu.get_barrier_semaphore()
    for d in range(1, n):
        pl.semaphore_signal(
            barrier, 1, device_id=_peer(axis, other, (me + d) % n), device_id_type=MESH_ID
        )
    pl.semaphore_wait(barrier, n - 1)
    gathers = []
    for d in range(1, n):
        c = pltpu.make_async_remote_copy(
            x_ref, gath.at[d], s2.at[d], r2.at[d],
            device_id=_peer(axis, other, (me + d) % n), device_id_type=MESH_ID,
        )
        c.start()
        gathers.append(c)
    o_ref[pl.ds(pl.multiple_of(me * ch, ch), ch), :] = x_ref[...]
    for d, c in enumerate(gathers, 1):
        c.wait()
        src = pl.multiple_of(((me - d + n) % n) * ch, ch)
        o_ref[pl.ds(src, ch), :] = gath[d]


def all_gather(x, axis, other, n, collective_id):
    ch, lanes = x.shape
    return pl.pallas_call(
        functools.partial(_gather_kernel, axis, other, n),
        out_shape=jax.ShapeDtypeStruct((n * ch, lanes), x.dtype),
        in_specs=[pl.BlockSpec(memory_space=pltpu.VMEM)],
        out_specs=pl.BlockSpec(memory_space=pltpu.VMEM),
        scratch_shapes=[
            pltpu.VMEM((n, ch, lanes), x.dtype),
            pltpu.SemaphoreType.DMA((n,)),
            pltpu.SemaphoreType.DMA((n,)),
        ],
        compiler_params=pltpu.CompilerParams(collective_id=collective_id, has_side_effects=True),
    )(x)


def _forward_kernel(n, ch, x_ref, mass_ref, o_ref, recv, mine, gath, s1, r1, s2, r2):
    axis, other = "col", "row"
    me = lax.axis_index(axis)
    barrier = pltpu.get_barrier_semaphore()
    for d in range(1, n):
        pl.semaphore_signal(
            barrier, 1, device_id=_peer(axis, other, (me + d) % n), device_id_type=MESH_ID
        )
    pl.semaphore_wait(barrier, n - 1)
    sends = []
    for d in range(1, n):
        peer = (me + d) % n
        start = pl.multiple_of(peer * ch, ch)
        c = pltpu.make_async_remote_copy(
            x_ref.at[pl.ds(start, ch)], recv.at[d], s1.at[d], r1.at[d],
            device_id=_peer(axis, other, peer), device_id_type=MESH_ID,
        )
        c.start()
        sends.append(c)
    own = pl.multiple_of(me * ch, ch)
    acc = x_ref[pl.ds(own, ch), :]
    for d, c in enumerate(sends, 1):
        c.wait()
        acc = acc + recv[d]
    mine[...] = (acc * mass_ref[...]).astype(mine.dtype)
    gathers = []
    for d in range(1, n):
        c = pltpu.make_async_remote_copy(
            mine, gath.at[d], s2.at[d], r2.at[d],
            device_id=_peer(axis, other, (me + d) % n), device_id_type=MESH_ID,
        )
        c.start()
        gathers.append(c)
    o_ref[pl.ds(own, ch), :] = mine[...]
    for d, c in enumerate(gathers, 1):
        c.wait()
        src = pl.multiple_of(((me - d + n) % n) * ch, ch)
        o_ref[pl.ds(src, ch), :] = gath[d]


def forward_reduce(x, mass, n, collective_id):
    rows, lanes = x.shape
    ch = rows // n
    return pl.pallas_call(
        functools.partial(_forward_kernel, n, ch),
        out_shape=jax.ShapeDtypeStruct(x.shape, jnp.bfloat16),
        in_specs=[pl.BlockSpec(memory_space=pltpu.VMEM)] * 2,
        out_specs=pl.BlockSpec(memory_space=pltpu.VMEM),
        scratch_shapes=[
            pltpu.VMEM((n, ch, lanes), x.dtype),
            pltpu.VMEM((ch, lanes), jnp.bfloat16),
            pltpu.VMEM((n, ch, lanes), jnp.bfloat16),
            pltpu.SemaphoreType.DMA((n,)),
            pltpu.SemaphoreType.DMA((n,)),
            pltpu.SemaphoreType.DMA((n,)),
            pltpu.SemaphoreType.DMA((n,)),
        ],
        compiler_params=pltpu.CompilerParams(collective_id=collective_id, has_side_effects=True),
    )(x, mass)


def _gather2_kernel(axis, other, n, x_ref, y_ref, o_ref, p_ref, gx, gy, sx, rx, sy, ry):
    me = lax.axis_index(axis)
    cx = x_ref.shape[0]
    cy = y_ref.shape[0]
    barrier = pltpu.get_barrier_semaphore()
    for d in range(1, n):
        pl.semaphore_signal(
            barrier, 1, device_id=_peer(axis, other, (me + d) % n), device_id_type=MESH_ID
        )
    pl.semaphore_wait(barrier, n - 1)
    copies = []
    for d in range(1, n):
        peer = _peer(axis, other, (me + d) % n)
        a = pltpu.make_async_remote_copy(
            x_ref, gx.at[d], sx.at[d], rx.at[d], device_id=peer, device_id_type=MESH_ID
        )
        b = pltpu.make_async_remote_copy(
            y_ref, gy.at[d], sy.at[d], ry.at[d], device_id=peer, device_id_type=MESH_ID
        )
        a.start()
        b.start()
        copies.append((a, b))
    o_ref[pl.ds(pl.multiple_of(me * cx, cx), cx), :] = x_ref[...]
    p_ref[pl.ds(pl.multiple_of(me * cy, cy), cy), :] = y_ref[...]
    for d, (a, b) in enumerate(copies, 1):
        a.wait()
        b.wait()
        src = (me - d + n) % n
        o_ref[pl.ds(pl.multiple_of(src * cx, cx), cx), :] = gx[d]
        p_ref[pl.ds(pl.multiple_of(src * cy, cy), cy), :] = gy[d]


def all_gather2(x, y, axis, other, n, collective_id):
    return pl.pallas_call(
        functools.partial(_gather2_kernel, axis, other, n),
        out_shape=(
            jax.ShapeDtypeStruct((n * x.shape[0], x.shape[1]), x.dtype),
            jax.ShapeDtypeStruct((n * y.shape[0], y.shape[1]), y.dtype),
        ),
        in_specs=[pl.BlockSpec(memory_space=pltpu.VMEM)] * 2,
        out_specs=(pl.BlockSpec(memory_space=pltpu.VMEM),) * 2,
        scratch_shapes=[
            pltpu.VMEM((n,) + x.shape, x.dtype),
            pltpu.VMEM((n,) + y.shape, y.dtype),
            pltpu.SemaphoreType.DMA((n,)),
            pltpu.SemaphoreType.DMA((n,)),
            pltpu.SemaphoreType.DMA((n,)),
            pltpu.SemaphoreType.DMA((n,)),
        ],
        compiler_params=pltpu.CompilerParams(collective_id=collective_id, has_side_effects=True),
    )(x, y)


def _gram_of(a):
    return lax.dot_general(
        a, a, (((1,), (1,)), ((), ())), precision=lax.Precision.HIGHEST,
        preferred_element_type=jnp.float32,
    )


def _backward_kernel(n, m, x_ref, icol_ref, o_ref, g_ref, recv, gath, g3, s1, r1, s2, r2, s3, r3):
    me = lax.axis_index("row")
    mc = lax.axis_index("col")
    barrier = pltpu.get_barrier_semaphore()
    for d in range(1, n):
        pl.semaphore_signal(barrier, 1, device_id=((me + d) % n, mc), device_id_type=MESH_ID)
    for d in range(1, m):
        pl.semaphore_signal(barrier, 1, device_id=(me, (mc + d) % m), device_id_type=MESH_ID)
    pl.semaphore_wait(barrier, n - 1 + m - 1)
    sends = []
    for d in range(1, n):
        peer = (me + d) % n
        c = pltpu.make_async_remote_copy(
            x_ref.at[peer], recv.at[d], s1.at[d], r1.at[d],
            device_id=(peer, mc), device_id_type=MESH_ID,
        )
        c.start()
        sends.append(c)
    acc = x_ref[me]
    for d, c in enumerate(sends, 1):
        c.wait()
        acc = acc + recv[d]
    gath[0] = acc * icol_ref[...]
    gathers = []
    for d in range(1, n):
        c = pltpu.make_async_remote_copy(
            gath.at[0], gath.at[d], s2.at[d], r2.at[d],
            device_id=((me + d) % n, mc), device_id_type=MESH_ID,
        )
        c.start()
        gathers.append(c)
    for c in gathers:
        c.wait()
    g = None
    for p in range(n):
        chunk = gath[(me - p + n) % n]
        o_ref[p] = chunk
        term = _gram_of(chunk)
        g = term if g is None else g + term
    g3[0] = g
    grams = []
    for d in range(1, m):
        c = pltpu.make_async_remote_copy(
            g3.at[0], g3.at[d], s3.at[d], r3.at[d],
            device_id=(me, (mc + d) % m), device_id_type=MESH_ID,
        )
        c.start()
        grams.append(c)
    for c in grams:
        c.wait()
    total = g3[mc % m]
    for q in range(1, m):
        total = total + g3[(mc - q + m) % m]
    g_ref[...] = total


def backward_reduce(x, icol, n, m, collective_id):
    chunks, vecs, lanes = x.shape
    return pl.pallas_call(
        functools.partial(_backward_kernel, n, m),
        out_shape=(
            jax.ShapeDtypeStruct(x.shape, jnp.float32),
            jax.ShapeDtypeStruct((vecs, vecs), jnp.float32),
        ),
        in_specs=[pl.BlockSpec(memory_space=pltpu.VMEM)] * 2,
        out_specs=(pl.BlockSpec(memory_space=pltpu.VMEM),) * 2,
        scratch_shapes=[
            pltpu.VMEM((n, vecs, lanes), jnp.float32),
            pltpu.VMEM((n, vecs, lanes), jnp.float32),
            pltpu.VMEM((m, vecs, vecs), jnp.float32),
            pltpu.SemaphoreType.DMA((n,)),
            pltpu.SemaphoreType.DMA((n,)),
            pltpu.SemaphoreType.DMA((n,)),
            pltpu.SemaphoreType.DMA((n,)),
            pltpu.SemaphoreType.DMA((m,)),
            pltpu.SemaphoreType.DMA((m,)),
        ],
        compiler_params=pltpu.CompilerParams(collective_id=collective_id, has_side_effects=True),
    )(x, icol)


def all_reduce(x, axis, other, n, collective_id, two_phase=True):
    rows, lanes = x.shape
    ch = rows // n if two_phase else rows
    slots = ch if two_phase else rows
    return pl.pallas_call(
        functools.partial(_reduce_kernel, axis, other, n, ch, two_phase),
        out_shape=jax.ShapeDtypeStruct(x.shape, x.dtype),
        in_specs=[pl.BlockSpec(memory_space=pltpu.VMEM)],
        out_specs=pl.BlockSpec(memory_space=pltpu.VMEM),
        scratch_shapes=[
            pltpu.VMEM((n, slots, lanes), x.dtype),
            pltpu.VMEM((ch, lanes), x.dtype),
            pltpu.VMEM((n, ch, lanes), x.dtype),
            pltpu.SemaphoreType.DMA((n,)),
            pltpu.SemaphoreType.DMA((n,)),
            pltpu.SemaphoreType.DMA((n,)),
            pltpu.SemaphoreType.DMA((n,)),
        ],
        compiler_params=pltpu.CompilerParams(collective_id=collective_id, has_side_effects=True),
    )(x)


def rotate(projected, gram):
    lower = jnp.linalg.cholesky(gram)
    inverse = lax.linalg.triangular_solve(
        lower, jnp.eye(gram.shape[0], dtype=jnp.float32), left_side=True, lower=True
    )
    return jnp.einsum(
        "kl,bli->bki",
        inverse,
        projected,
        precision=lax.Precision.HIGHEST,
        preferred_element_type=jnp.float32,
    )


def rotate_pairs(projected, gram):
    lower = jnp.linalg.cholesky(gram)
    inverse = lax.linalg.triangular_solve(
        lower, jnp.eye(gram.shape[0], dtype=jnp.float32), left_side=True, lower=True
    )
    return jnp.einsum(
        "kl,plx->pkx",
        inverse,
        projected,
        precision=lax.Precision.HIGHEST,
        preferred_element_type=jnp.float32,
    )


def local_gram(projected):
    return jnp.einsum(
        "bki,bli->kl",
        projected,
        projected,
        precision=lax.Precision.HIGHEST,
        preferred_element_type=jnp.float32,
    )


def panel_sum(partial, axis, other, n, collective_id):
    blocks, vecs, bsize = partial.shape
    flat = partial.reshape(blocks * vecs * bsize // LANES, LANES)
    return all_reduce(flat, axis, other, n, collective_id).reshape(blocks, vecs, bsize)


def per_device(blocks, block_row, block_col, counts, vectors, row_mass, col_mass):
    tile = blocks[0, 0]
    n_cap = tile.shape[0]
    bsize = row_mass.shape[1]
    vecs = vectors.shape[1] // bsize
    own = vectors.shape[0]
    n_row = lax.axis_size("row")
    n_col = lax.axis_size("col")
    row_panel = own * n_col
    col_panel = own * n_row
    total_boxes = float(own * bsize * n_row * n_col)
    rows_idx = block_row[0, 0]
    cols_idx = block_col[0, 0]
    live = jnp.arange(n_cap) < counts[0, 0]
    fwd_ids = jnp.where(live, rows_idx, row_panel)
    bwd_ids = jnp.where(live, cols_idx, col_panel)
    square = tile.reshape(n_cap, bsize, bsize)
    vec_rows = own * vecs * bsize // LANES
    own_inv = 1.0 / jnp.sqrt(col_mass)
    first = (vectors.reshape(own, vecs, bsize) * own_inv[:, None, :]).astype(jnp.bfloat16)
    mass_pad = jnp.zeros((8, 128), jnp.float32).at[0, : own * bsize].set(col_mass.reshape(-1))
    got, mass_got = all_gather2(first.reshape(vec_rows, LANES), mass_pad, "row", "col", n_row, 4)
    first_panel = got.reshape(col_panel, vecs, bsize)
    col_mass_panel = mass_got.reshape(n_row, 8, 128)[:, 0, : own * bsize].reshape(col_panel, bsize)
    inv_col = 1.0 / jnp.sqrt(col_mass_panel)
    pairs = col_panel // 2
    inv_pairs = inv_col.reshape(pairs, 1, 2 * bsize)
    own_pair = jnp.broadcast_to(own_inv.reshape(1, own * bsize), (vecs, own * bsize))
    row_mass_spread = jnp.broadcast_to(row_mass[:, None, :], (own, vecs, bsize)).reshape(vec_rows, LANES)
    fwd_hot = (fwd_ids[None, :] == jnp.arange(row_panel)[:, None]).astype(jnp.float32)
    bwd_hot = (bwd_ids[None, :] == jnp.arange(col_panel)[:, None]).astype(jnp.float32)
    for step in range(ITERS):
        if step == 0:
            scaled = first_panel
        else:
            paired = (current * inv_pairs).astype(jnp.bfloat16)
            scaled = paired.reshape(pairs, vecs, 2, bsize).transpose(0, 2, 1, 3).reshape(col_panel, vecs, bsize)
        forward_taken = jnp.take(scaled, cols_idx, axis=0)
        forward_product = jnp.einsum(
            "bij,bkj->bki", square, forward_taken, preferred_element_type=jnp.float32
        )
        forward_summed = jnp.einsum(
            "rs,ski->rki", fwd_hot, forward_product, precision=lax.Precision.HIGHEST,
            preferred_element_type=jnp.float32,
        )
        flat = forward_summed.reshape(row_panel * vecs * bsize // LANES, LANES)
        weighted = forward_reduce(flat, row_mass_spread, n_col, 1).reshape(row_panel, vecs, bsize)
        taken = jnp.take(weighted, rows_idx, axis=0)
        product = jnp.einsum("bij,bki->bkj", square, taken, preferred_element_type=jnp.float32)
        summed = jnp.einsum(
            "pbs,skj->pkbj", bwd_hot.reshape(pairs, 2, n_cap), product,
            precision=lax.Precision.HIGHEST, preferred_element_type=jnp.float32,
        ).reshape(pairs, vecs, 2 * bsize)
        projected, gram = backward_reduce(summed, own_pair, n_row, n_col, 2)
        current = rotate_pairs(projected, gram / total_boxes)
    me = lax.axis_index("row")
    mine = lax.dynamic_index_in_dim(current, me, 0, keepdims=False)
    return mine.reshape(vecs, own, bsize).transpose(1, 0, 2).reshape(own, vecs * bsize)


def solution(mesh):
    in_specs = (
        P("row", "col", None, None),
        P("row", "col", None),
        P("row", "col", None),
        P("row", "col"),
        P(("col", "row"), None),
        P(("row", "col"), None),
        P(("col", "row"), None),
    )
    out_specs = P(("col", "row"), None)
    return jax.shard_map(
        per_device, mesh=mesh, in_specs=in_specs, out_specs=out_specs, check_vma=False
    )
```

profile of v0, /device:TPU:1, one launch (start us, length us, event | category | flops | bytes accessed | tf_op | source)
XLA Modules:
  0.0 350.3 jit_solution(7416243531381722495)
XLA Ops:
  8.4 13.3 %shard_map.73 = (bf16[256,512]{1,0:T(8,128)(2,1)}, f32[128,128]{1,0:T(8,128)}) custom-call(bf16[16,512]{1,0:T(8,128)(2,1)} %multiply_convert_fusion.x_ref, f32[8,128]{1,0:T(8,128)} %scatter.4.y_ref), custom_call_target="tpu_custom_call" | custom-call | tf_op jit(solution)/shard_map/pallas_call | solution.py:210
  29.6 4.8 %copy.43 = bf16[128,64,64]{1,2,0:T(8,128)(2,1)} copy(bf16[128,64,64]{0,2,1:T(8,128)(2,1)S(1)} %bitcast.122) | data formatting | bytes 2097152 | tf_op jit(solution)/shard_map/reshape;squeeze | solution.py:400
  37.3 3.8 %fusion.14 = f32[16,64,64]{2,0,1:T(8,128)S(1)} fusion(f32[128,64,64]{2,1,0:T(8,128)S(1)} %fusion.26, s32[128]{0:T(128)S(1)} %get-tuple-element.50), kind=kOutput, calls=%fused_computation.22 | convolution fusion | flops 100665344 | bytes 2359808 | tf_op jit(solution)/shard_map/rs,ski->rki/dot_general | solution.py:425
  42.2 16.3 %shard_map.74 = bf16[128,512]{1,0:T(8,128)(2,1)} custom-call(f32[128,512]{1,0:T(8,128)} %reshape.164.x_ref, f32[16,512]{1,0:T(8,128)} %reshape.165.mass_ref), custom_call_target="tpu_custom_call" | custom-call | tf_op jit(solution)/shard_map/pallas_call | solution.py:159
  64.1 3.9 %fusion.36 = f32[16,64,2,64]{3,0,2,1:T(8,128)S(1)} fusion(f32[128,64,64,1]{2,1,0,3:T(8,128)S(1)} %convolution_bitcast_fusion.3, s32[16,2]{0,1:T(2,128)S(1)} %multiply_add_fusion, s32[128]{0:T(128)S(1)} %get-tuple-element.52), kind=kOutput, calls=%fused_computation.48 | convolution fusion | flops 201330688 | bytes 2622080 | tf_op jit(solution)/shard_map/pbs,skj->pkbj/dot_general | solution.py:433
  70.0 28.8 %shard_map.75 = (f32[16,64,128]{2,1,0:T(8,128)}, f32[64,64]{1,0:T(8,128)}) custom-call(f32[16,64,128]{2,1,0:T(8,128)} %reshape.167.x_ref, f32[64,128]{1,0:T(8,128)} %broadcast_in_dim.49.icol_ref), custom_call_target="tpu_custom_call" | custom-call | tf_op jit(solution)/shard_map/pallas_call | solution.py:295
  99.8 5.8 %cholesky.74 = f32[64,64]{1,0:T(8,128)S(1)} custom-call(f32[64,64]{1,0:T(8,128)S(1)} %fusion.77), custom_call_target="Cholesky" | custom-call | tf_op jit(solution)/shard_map/jit(cholesky)/cholesky | solution.py:355
  107.0 4.9 %custom-call.8 = f32[1,64,64]{1,2,0:T(8,128)S(1)} custom-call(f32[1,64,64]{2,1,0:T(8,128)S(1)} %fusion.66), custom_call_target="InvertDiagBlocksLowerTriangular" | custom-call | tf_op jit(solution)/shard_map/triangular_solve/custom-call.0 | solution.py:356
  124.0 13.4 %shard_map.76 = bf16[128,512]{1,0:T(8,128)(2,1)} custom-call(f32[128,512]{1,0:T(8,128)} %reshape.170.x_ref, f32[16,512]{1,0:T(8,128)} %reshape.165.mass_ref), custom_call_target="tpu_custom_call" | custom-call | tf_op jit(solution)/shard_map/pallas_call | solution.py:159
  143.0 4.1 %fusion.39 = f32[16,64,2,64]{3,0,2,1:T(8,128)S(1)} fusion(f32[128,64,64,1]{2,1,0,3:T(8,128)S(1)} %convolution_bitcast_fusion.2, s32[16,2]{0,1:T(2,128)S(1)} %multiply_add_fusion, s32[128]{0:T(128)S(1)} %get-tuple-element.52), kind=kOutput, calls=%fused_computation.49 | convolution fusion | flops 201330688 | bytes 2622080 | tf_op jit(solution)/shard_map/pbs,skj->pkbj/dot_general | solution.py:433
  149.1 27.9 %shard_map.77 = (f32[16,64,128]{2,1,0:T(8,128)}, f32[64,64]{1,0:T(8,128)}) custom-call(f32[16,64,128]{2,1,0:T(8,128)} %reshape.172.x_ref, f32[64,128]{1,0:T(8,128)} %broadcast_in_dim.49.icol_ref), custom_call_target="tpu_custom_call" | custom-call | tf_op jit(solution)/shard_map/pallas_call | solution.py:295
  177.9 5.8 %cholesky.85 = f32[64,64]{1,0:T(8,128)S(1)} custom-call(f32[64,64]{1,0:T(8,128)S(1)} %fusion.75), custom_call_target="Cholesky" | custom-call | tf_op jit(solution)/shard_map/jit(cholesky)/cholesky | solution.py:355
  185.1 4.9 %custom-call.9 = f32[1,64,64]{1,2,0:T(8,128)S(1)} custom-call(f32[1,64,64]{2,1,0:T(8,128)S(1)} %fusion.67), custom_call_target="InvertDiagBlocksLowerTriangular" | custom-call | tf_op jit(solution)/shard_map/triangular_solve/custom-call.0 | solution.py:356
  197.3 4.0 %fusion.10 = f32[16,64,64]{2,0,1:T(8,128)S(1)} fusion(f32[128,64,64]{2,1,0:T(8,128)S(1)} %fusion.20, s32[128]{0:T(128)S(1)} %get-tuple-element.50), kind=kOutput, calls=%fused_computation.18 | convolution fusion | flops 100665344 | bytes 2359808 | tf_op jit(solution)/shard_map/rs,ski->rki/dot_general | solution.py:425
  202.4 13.7 %shard_map.78 = bf16[128,512]{1,0:T(8,128)(2,1)} custom-call(f32[128,512]{1,0:T(8,128)} %reshape.174.x_ref, f32[16,512]{1,0:T(8,128)} %reshape.165.mass_ref), custom_call_target="tpu_custom_call" | custom-call | tf_op jit(solution)/shard_map/pallas_call | solution.py:159
  221.6 3.9 %fusion.42 = f32[16,64,2,64]{3,0,2,1:T(8,128)S(1)} fusion(f32[128,64,64,1]{2,1,0,3:T(8,128)S(1)} %convolution_bitcast_fusion.1, s32[16,2]{0,1:T(2,128)S(1)} %multiply_add_fusion, s32[128]{0:T(128)S(1)} %get-tuple-element.52), kind=kOutput, calls=%fused_computation.50 | convolution fusion | flops 201330688 | bytes 2622080 | tf_op jit(solution)/shard_map/pbs,skj->pkbj/dot_general | solution.py:433
  227.5 28.1 %shard_map.79 = (f32[16,64,128]{2,1,0:T(8,128)}, f32[64,64]{1,0:T(8,128)}) custom-call(f32[16,64,128]{2,1,0:T(8,128)} %reshape.176.x_ref, f32[64,128]{1,0:T(8,128)} %broadcast_in_dim.49.icol_ref), custom_call_target="tpu_custom_call" | custom-call | tf_op jit(solution)/shard_map/pallas_call | solution.py:295
  256.5 5.8 %cholesky.96 = f32[64,64]{1,0:T(8,128)S(1)} custom-call(f32[64,64]{1,0:T(8,128)S(1)} %fusion.73), custom_call_target="Cholesky" | custom-call | tf_op jit(solution)/shard_map/jit(cholesky)/cholesky | solution.py:355
  263.7 4.9 %custom-call.10 = f32[1,64,64]{1,2,0:T(8,128)S(1)} custom-call(f32[1,64,64]{2,1,0:T(8,128)S(1)} %fusion.68), custom_call_target="InvertDiagBlocksLowerTriangular" | custom-call | tf_op jit(solution)/shard_map/triangular_solve/custom-call.0 | solution.py:356
  281.1 13.0 %shard_map.80 = bf16[128,512]{1,0:T(8,128)(2,1)} custom-call(f32[128,512]{1,0:T(8,128)} %reshape.178.x_ref, f32[16,512]{1,0:T(8,128)} %reshape.165.mass_ref), custom_call_target="tpu_custom_call" | custom-call | tf_op jit(solution)/shard_map/pallas_call | solution.py:159
  299.8 3.9 %fusion.45 = f32[16,64,2,64]{3,0,2,1:T(8,128)S(1)} fusion(f32[128,64,64,1]{2,1,0,3:T(8,128)S(1)} %convolution_bitcast_fusion, s32[16,2]{0,1:T(2,128)S(1)} %multiply_add_fusion, s32[128]{0:T(128)S(1)} %get-tuple-element.52), kind=kOutput, calls=%fused_computation.51 | convolution fusion | flops 201330688 | bytes 2622080 | tf_op jit(solution)/shard_map/pbs,skj->pkbj/dot_general | solution.py:433
  305.8 28.5 %shard_map.81 = (f32[16,64,128]{2,1,0:T(8,128)}, f32[64,64]{1,0:T(8,128)}) custom-call(f32[16,64,128]{2,1,0:T(8,128)} %reshape.180.x_ref, f32[64,128]{1,0:T(8,128)} %broadcast_in_dim.49.icol_ref), custom_call_target="tpu_custom_call" | custom-call | tf_op jit(solution)/shard_map/pallas_call | solution.py:295
  335.3 5.8 %cholesky.107 = f32[64,64]{1,0:T(8,128)S(1)} custom-call(f32[64,64]{1,0:T(8,128)S(1)} %fusion.71), custom_call_target="Cholesky" | custom-call | tf_op jit(solution)/shard_map/jit(cholesky)/cholesky | solution.py:355
  342.5 4.9 %custom-call.11 = f32[1,64,64]{1,2,0:T(8,128)S(1)} custom-call(f32[1,64,64]{2,1,0:T(8,128)S(1)} %fusion.69), custom_call_target="InvertDiagBlocksLowerTriangular" | custom-call | tf_op jit(solution)/shard_map/triangular_solve/custom-call.0 | solution.py:356
  (107 shorter events, 94.4 us)
Async XLA Ops:
  0.0 23.8 %copy-start = (bf16[1,1,128,4096]{3,2,1,0:T(8,128)(2,1)S(1)}, bf16[1,1,128,4096]{3,2,1,0:T(8,128)(2,1)}, u32[]{:S(2)}) copy-start(bf16[1,1,128,4096]{3,2,1,0:T(8,128)(2,1)} %param.16) | copy-start | bytes 3145732
where the time goes:
time: 355 us; the launch traced here: 350 us
  Pallas kernels  183 us (52%)
  matrix products  60.6 us (17%)
  local copies, waits for them, and re-layouts  53.9 us (15%)
  other arithmetic  51.3 us (14%)
    pallas_call x4, Pallas kernels, backward_reduce(): pl.pallas_call(functools.partial(_backward_kernel, n, m), out_shape=(jax....  113 us
    pallas_call x4, Pallas kernels, forward_reduce(): pl.pallas_call(functools.partial(_forward_kernel, n, ch), out_shape=jax.S...  56.4 us
    another operation x12, other arithmetic, rotate_pairs(): lower = jnp.linalg.cholesky(gram)  26.1 us
    another operation x8, other arithmetic, rotate_pairs(): lax.linalg.triangular_solve(lower, jnp.eye(gram.shape[0], dtype=jnp.float...  22.1 us
    dot_general x4, matrix products, per_device(): jnp.einsum('pbs,skj->pkbj', bwd_hot.reshape(pairs, 2, n_cap), product, pr...  15.8 us
    dot_general x4, matrix products, per_device(): jnp.einsum('rs,ski->rki', fwd_hot, forward_product, precision=lax.Precisi...  15.6 us
    pallas_call x1, Pallas kernels, all_gather2(): pl.pallas_call(functools.partial(_gather2_kernel, axis, other, n), out_sh...  13.3 us
    dot_general x4, matrix products, per_device(): jnp.einsum('bij,bkj->bki', square, forward_taken, preferred_element_type=...  11.9 us

commit v1 on v0

--- a/solution.py
+++ b/solution.py
@@ -423,7 +423,7 @@
             "bij,bkj->bki", square, forward_taken, preferred_element_type=jnp.float32
         )
         forward_summed = jnp.einsum(
-            "rs,ski->rki", fwd_hot, forward_product, precision=lax.Precision.HIGHEST,
+            "rs,ski->rki", fwd_hot, forward_product, precision=lax.Precision.HIGH,
             preferred_element_type=jnp.float32,
         )
         flat = forward_summed.reshape(row_panel * vecs * bsize // LANES, LANES)
@@ -432,7 +432,7 @@
         product = jnp.einsum("bij,bki->bkj", square, taken, preferred_element_type=jnp.float32)
         summed = jnp.einsum(
             "pbs,skj->pkbj", bwd_hot.reshape(pairs, 2, n_cap), product,
-            precision=lax.Precision.HIGHEST, preferred_element_type=jnp.float32,
+            precision=lax.Precision.HIGH, preferred_element_type=jnp.float32,
         ).reshape(pairs, vecs, 2 * bsize)
         projected, gram = backward_reduce(summed, own_pair, n_row, n_col, 2)
         current = rotate_pairs(projected, gram / total_boxes)

time: 355 us -> 350 us (0.986)
  matrix products: 60.6 us -> 54.4 us
where the time goes in v1:
time: 350 us; the launch traced here: 344 us
  Pallas kernels  183 us (52%)
  matrix products  54.4 us (16%)
  local copies, waits for them, and re-layouts  53.8 us (15%)
  other arithmetic  51.7 us (15%)
    pallas_call x4, Pallas kernels, backward_reduce(): pl.pallas_call(functools.partial(_backward_kernel, n, m), out_shape=(jax....  113 us
    pallas_call x4, Pallas kernels, forward_reduce(): pl.pallas_call(functools.partial(_forward_kernel, n, ch), out_shape=jax.S...  56.3 us
    another operation x12, other arithmetic, rotate_pairs(): lower = jnp.linalg.cholesky(gram)  26.5 us
    another operation x8, other arithmetic, rotate_pairs(): lax.linalg.triangular_solve(lower, jnp.eye(gram.shape[0], dtype=jnp.float...  22.1 us
    pallas_call x1, Pallas kernels, all_gather2(): pl.pallas_call(functools.partial(_gather2_kernel, axis, other, n), out_sh...  13.3 us
    dot_general x4, matrix products, per_device(): jnp.einsum('pbs,skj->pkbj', bwd_hot.reshape(pairs, 2, n_cap), product, pr...  13 us
    dot_general x4, matrix products, per_device(): jnp.einsum('rs,ski->rki', fwd_hot, forward_product, precision=lax.Precisi...  12.6 us
    dot_general x4, matrix products, per_device(): jnp.einsum('bij,bkj->bki', square, forward_taken, preferred_element_type=...  11.9 us

profile of v1, /device:TPU:1, one launch (start us, length us, event | category | flops | bytes accessed | tf_op | source)
XLA Modules:
  0.0 344.4 jit_solution(2276614751159971967)
XLA Ops:
  8.4 13.3 %shard_map.73 = (bf16[256,512]{1,0:T(8,128)(2,1)}, f32[128,128]{1,0:T(8,128)}) custom-call(bf16[16,512]{1,0:T(8,128)(2,1)} %multiply_convert_fusion.x_ref, f32[8,128]{1,0:T(8,128)} %scatter.4.y_ref), custom_call_target="tpu_custom_call" | custom-call | tf_op jit(solution)/shard_map/pallas_call | solution.py:210
  29.6 4.7 %copy.43 = bf16[128,64,64]{1,2,0:T(8,128)(2,1)} copy(bf16[128,64,64]{0,2,1:T(8,128)(2,1)S(1)} %bitcast.122) | data formatting | bytes 2097152 | tf_op jit(solution)/shard_map/reshape;squeeze | solution.py:400
  37.2 3.1 fusion.14
  41.4 16.3 %shard_map.74 = bf16[128,512]{1,0:T(8,128)(2,1)} custom-call(f32[128,512]{1,0:T(8,128)} %reshape.164.x_ref, f32[16,512]{1,0:T(8,128)} %reshape.165.mass_ref), custom_call_target="tpu_custom_call" | custom-call | tf_op jit(solution)/shard_map/pallas_call | solution.py:159
  63.3 3.2 fusion.36
  68.5 28.8 %shard_map.75 = (f32[16,64,128]{2,1,0:T(8,128)}, f32[64,64]{1,0:T(8,128)}) custom-call(f32[16,64,128]{2,1,0:T(8,128)} %reshape.167.x_ref, f32[64,128]{1,0:T(8,128)} %broadcast_in_dim.49.icol_ref), custom_call_target="tpu_custom_call" | custom-call | tf_op jit(solution)/shard_map/pallas_call | solution.py:295
  98.2 6.2 %cholesky.74 = f32[64,64]{1,0:T(8,128)S(1)} custom-call(f32[64,64]{1,0:T(8,128)S(1)} %fusion.77), custom_call_target="Cholesky" | custom-call | tf_op jit(solution)/shard_map/jit(cholesky)/cholesky | solution.py:355
  105.8 4.9 %custom-call.8 = f32[1,64,64]{1,2,0:T(8,128)S(1)} custom-call(f32[1,64,64]{2,1,0:T(8,128)S(1)} %fusion.66), custom_call_target="InvertDiagBlocksLowerTriangular" | custom-call | tf_op jit(solution)/shard_map/triangular_solve/custom-call.0 | solution.py:356
  122.1 13.4 %shard_map.76 = bf16[128,512]{1,0:T(8,128)(2,1)} custom-call(f32[128,512]{1,0:T(8,128)} %reshape.170.x_ref, f32[16,512]{1,0:T(8,128)} %reshape.165.mass_ref), custom_call_target="tpu_custom_call" | custom-call | tf_op jit(solution)/shard_map/pallas_call | solution.py:159
  141.1 3.2 fusion.39
  146.4 27.9 %shard_map.77 = (f32[16,64,128]{2,1,0:T(8,128)}, f32[64,64]{1,0:T(8,128)}) custom-call(f32[16,64,128]{2,1,0:T(8,128)} %reshape.172.x_ref, f32[64,128]{1,0:T(8,128)} %broadcast_in_dim.49.icol_ref), custom_call_target="tpu_custom_call" | custom-call | tf_op jit(solution)/shard_map/pallas_call | solution.py:295
  175.3 5.8 %cholesky.85 = f32[64,64]{1,0:T(8,128)S(1)} custom-call(f32[64,64]{1,0:T(8,128)S(1)} %fusion.75), custom_call_target="Cholesky" | custom-call | tf_op jit(solution)/shard_map/jit(cholesky)/cholesky | solution.py:355
  182.5 4.9 %custom-call.9 = f32[1,64,64]{1,2,0:T(8,128)S(1)} custom-call(f32[1,64,64]{2,1,0:T(8,128)S(1)} %fusion.67), custom_call_target="InvertDiagBlocksLowerTriangular" | custom-call | tf_op jit(solution)/shard_map/triangular_solve/custom-call.0 | solution.py:356
  198.8 13.6 %shard_map.78 = bf16[128,512]{1,0:T(8,128)(2,1)} custom-call(f32[128,512]{1,0:T(8,128)} %reshape.174.x_ref, f32[16,512]{1,0:T(8,128)} %reshape.165.mass_ref), custom_call_target="tpu_custom_call" | custom-call | tf_op jit(solution)/shard_map/pallas_call | solution.py:159
  218.0 3.4 fusion.42
  223.4 28.0 %shard_map.79 = (f32[16,64,128]{2,1,0:T(8,128)}, f32[64,64]{1,0:T(8,128)}) custom-call(f32[16,64,128]{2,1,0:T(8,128)} %reshape.176.x_ref, f32[64,128]{1,0:T(8,128)} %broadcast_in_dim.49.icol_ref), custom_call_target="tpu_custom_call" | custom-call | tf_op jit(solution)/shard_map/pallas_call | solution.py:295
  252.4 5.8 %cholesky.96 = f32[64,64]{1,0:T(8,128)S(1)} custom-call(f32[64,64]{1,0:T(8,128)S(1)} %fusion.73), custom_call_target="Cholesky" | custom-call | tf_op jit(solution)/shard_map/jit(cholesky)/cholesky | solution.py:355
  259.5 4.9 %custom-call.10 = f32[1,64,64]{1,2,0:T(8,128)S(1)} custom-call(f32[1,64,64]{2,1,0:T(8,128)S(1)} %fusion.68), custom_call_target="InvertDiagBlocksLowerTriangular" | custom-call | tf_op jit(solution)/shard_map/triangular_solve/custom-call.0 | solution.py:356
  271.7 3.3 fusion.8
  276.1 12.9 %shard_map.80 = bf16[128,512]{1,0:T(8,128)(2,1)} custom-call(f32[128,512]{1,0:T(8,128)} %reshape.178.x_ref, f32[16,512]{1,0:T(8,128)} %reshape.165.mass_ref), custom_call_target="tpu_custom_call" | custom-call | tf_op jit(solution)/shard_map/pallas_call | solution.py:159
  294.7 3.2 fusion.45
  299.8 28.4 %shard_map.81 = (f32[16,64,128]{2,1,0:T(8,128)}, f32[64,64]{1,0:T(8,128)}) custom-call(f32[16,64,128]{2,1,0:T(8,128)} %reshape.180.x_ref, f32[64,128]{1,0:T(8,128)} %broadcast_in_dim.49.icol_ref), custom_call_target="tpu_custom_call" | custom-call | tf_op jit(solution)/shard_map/pallas_call | solution.py:295
  329.1 5.8 %cholesky.107 = f32[64,64]{1,0:T(8,128)S(1)} custom-call(f32[64,64]{1,0:T(8,128)S(1)} %fusion.71), custom_call_target="Cholesky" | custom-call | tf_op jit(solution)/shard_map/jit(cholesky)/cholesky | solution.py:355
  336.3 4.9 %custom-call.11 = f32[1,64,64]{1,2,0:T(8,128)S(1)} custom-call(f32[1,64,64]{2,1,0:T(8,128)S(1)} %fusion.69), custom_call_target="InvertDiagBlocksLowerTriangular" | custom-call | tf_op jit(solution)/shard_map/triangular_solve/custom-call.0 | solution.py:356
  (107 shorter events, 92.5 us)
Async XLA Ops:
  0.0 23.8 %copy-start = (bf16[1,1,128,4096]{3,2,1,0:T(8,128)(2,1)S(1)}, bf16[1,1,128,4096]{3,2,1,0:T(8,128)(2,1)}, u32[]{:S(2)}) copy-start(bf16[1,1,128,4096]{3,2,1,0:T(8,128)(2,1)} %param.16) | copy-start | bytes 3145732

commit v2 on v1

--- a/solution.py
+++ b/solution.py
@@ -234,7 +234,32 @@
     )
 
 
-def _backward_kernel(n, m, x_ref, icol_ref, o_ref, g_ref, recv, gath, g3, s1, r1, s2, r2, s3, r3):
+def chol_inverse(a):
+    n = a.shape[0]
+    r = lax.broadcasted_iota(jnp.int32, (n, n), 0)
+    c = lax.broadcasted_iota(jnp.int32, (n, n), 1)
+    r1 = lax.broadcasted_iota(jnp.int32, (n, 1), 0)
+    c1 = lax.broadcasted_iota(jnp.int32, (1, n), 1)
+    x0 = jnp.where(r == c, 1.0, 0.0).astype(jnp.float32)
+
+    def step(j, carry):
+        m, x = carry
+        col = jnp.sum(jnp.where(c == j, m, 0.0), axis=1, keepdims=True)
+        row = jnp.sum(jnp.where(r == j, m, 0.0), axis=0, keepdims=True)
+        piv = jnp.sqrt(jnp.sum(jnp.where(r1 == j, col, 0.0), axis=0, keepdims=True))
+        lcol = jnp.where(r1 >= j, col / piv, 0.0)
+        lrow = jnp.where(c1 >= j, row / piv, 0.0)
+        m = m - lcol * lrow
+        xrow = jnp.sum(jnp.where(r == j, x, 0.0), axis=0, keepdims=True) / piv
+        x = jnp.where(r == j, xrow, x)
+        x = x - jnp.where(r1 > j, lcol, 0.0) * xrow
+        return m, x
+
+    m, x = lax.fori_loop(0, n, step, (a, x0))
+    return x
+
+
+def _backward_kernel(n, m, scale, x_ref, icol_ref, o_ref, recv, gath, g3, s1, r1, s2, r2, s3, r3):
     me = lax.axis_index("row")
     mc = lax.axis_index("col")
     barrier = pltpu.get_barrier_semaphore()
@@ -269,9 +294,7 @@
         c.wait()
     g = None
     for p in range(n):
-        chunk = gath[(me - p + n) % n]
-        o_ref[p] = chunk
-        term = _gram_of(chunk)
+        term = _gram_of(gath[(me - p + n) % n])
         g = term if g is None else g + term
     g3[0] = g
     grams = []
@@ -287,19 +310,21 @@
     total = g3[mc % m]
     for q in range(1, m):
         total = total + g3[(mc - q + m) % m]
-    g_ref[...] = total
-
-
-def backward_reduce(x, icol, n, m, collective_id):
+    inverse = chol_inverse(total * scale)
+    for p in range(n):
+        o_ref[p] = lax.dot_general(
+            inverse, gath[(me - p + n) % n], (((1,), (0,)), ((), ())),
+            precision=lax.Precision.HIGHEST, preferred_element_type=jnp.float32,
+        )
+
+
+def backward_reduce(x, icol, n, m, scale, collective_id):
     chunks, vecs, lanes = x.shape
     return pl.pallas_call(
-        functools.partial(_backward_kernel, n, m),
-        out_shape=(
-            jax.ShapeDtypeStruct(x.shape, jnp.float32),
-            jax.ShapeDtypeStruct((vecs, vecs), jnp.float32),
-        ),
+        functools.partial(_backward_kernel, n, m, scale),
+        out_shape=jax.ShapeDtypeStruct(x.shape, jnp.float32),
         in_specs=[pl.BlockSpec(memory_space=pltpu.VMEM)] * 2,
-        out_specs=(pl.BlockSpec(memory_space=pltpu.VMEM),) * 2,
+        out_specs=pl.BlockSpec(memory_space=pltpu.VMEM),
         scratch_shapes=[
             pltpu.VMEM((n, vecs, lanes), jnp.float32),
             pltpu.VMEM((n, vecs, lanes), jnp.float32),
@@ -434,8 +459,7 @@
             "pbs,skj->pkbj", bwd_hot.reshape(pairs, 2, n_cap), product,
             precision=lax.Precision.HIGH, preferred_element_type=jnp.float32,
         ).reshape(pairs, vecs, 2 * bsize)
-        projected, gram = backward_reduce(summed, own_pair, n_row, n_col, 2)
-        current = rotate_pairs(projected, gram / total_boxes)
+        current = backward_reduce(summed, own_pair, n_row, n_col, 1.0 / total_boxes, 2)
     me = lax.axis_index("row")
     mine = lax.dynamic_index_in_dim(current, me, 0, keepdims=False)
     return mine.reshape(vecs, own, bsize).transpose(1, 0, 2).reshape(own, vecs * bsize)

time: 350 us -> 325 us (0.929)
  other arithmetic: 51.7 us -> 6.31 us
  Pallas kernels: 183 us -> 219 us
  matrix products: 54.4 us -> 45.9 us
  local copies, waits for them, and re-layouts: 53.8 us -> 48.6 us
    another operation x23 -> x3, other arithmetic: 49 us -> 0.39 us  [the longest x12 26.5 us: rotate_pairs(): lower = jnp.linalg.cholesky(gram)]
    pallas_call x4, Pallas kernels: 113 us -> 150 us  [backward_reduce(): pl.pallas_call(functools.partial(_backward_kernel, n, m, scale), out_shap...]
    dot_general x4 -> x0, matrix products: 6.59 us -> none  [rotate_pairs(): jnp.einsum('kl,plx->pkx', inverse, projected, precision=lax.Precision.HIG...]
    another operation x2 -> x1, local copies, waits for them, and re-layouts: 7.66 us -> 4.11 us  [per_device(): square = tile.reshape(n_cap, bsize, bsize)]
where the time goes in v2:
time: 325 us; the launch traced here: 321 us
  Pallas kernels  219 us (67%)
  local copies, waits for them, and re-layouts  48.6 us (15%)
  matrix products  45.9 us (14%)
  other arithmetic  6.31 us (2%)
    pallas_call x4, Pallas kernels, backward_reduce(): pl.pallas_call(functools.partial(_backward_kernel, n, m, scale), out_shap...  150 us
    pallas_call x4, Pallas kernels, forward_reduce(): pl.pallas_call(functools.partial(_forward_kernel, n, ch), out_shape=jax.S...  56.1 us
    pallas_call x1, Pallas kernels, all_gather2(): pl.pallas_call(functools.partial(_gather2_kernel, axis, other, n), out_sh...  13.3 us
    dot_general x4, matrix products, per_device(): jnp.einsum('pbs,skj->pkbj', bwd_hot.reshape(pairs, 2, n_cap), product, pr...  12.7 us
    dot_general x4, matrix products, per_device(): jnp.einsum('rs,ski->rki', fwd_hot, forward_product, precision=lax.Precisi...  12.3 us
    dot_general x4, matrix products, per_device(): jnp.einsum('bij,bkj->bki', square, forward_taken, preferred_element_type=...  11.4 us
    dot_general x4, matrix products, per_device(): jnp.einsum('bij,bki->bkj', square, taken, preferred_element_type=jnp.floa...  9.37 us
    gather x4, local copies, waits for them, and re-layouts, per_device(): taken = jnp.take(weighted, rows_idx, axis=0)  8.62 us

profile of v2, /device:TPU:1, one launch (start us, length us, event | category | flops | bytes accessed | tf_op | source)
XLA Modules:
  0.0 321.2 jit_solution(18116432127220618952)
XLA Ops:
  8.4 13.3 %shard_map.73 = (bf16[256,512]{1,0:T(8,128)(2,1)}, f32[128,128]{1,0:T(8,128)}) custom-call(bf16[16,512]{1,0:T(8,128)(2,1)} %multiply_convert_fusion.3.x_ref, f32[8,128]{1,0:T(8,128)} %scatter.4.y_ref), custom_call_target="tpu_custom_call" | custom-call | tf_op jit(solution)/shard_map/pallas_call | solution.py:210
  25.1 4.1 %copy.28 = bf16[128,64,64]{2,1,0:T(8,128)(2,1)S(1)} copy(bf16[128,64,64]{0,2,1:T(8,128)(2,1)} %bitcast.63) | data formatting | bytes 2097152 | tf_op jit(solution)/shard_map/reshape;squeeze | solution.py:425
  31.4 2.9 fusion.26
  34.3 3.1 fusion.14
  38.4 16.3 %shard_map.74 = bf16[128,512]{1,0:T(8,128)(2,1)} custom-call(f32[128,512]{1,0:T(8,128)} %reshape.153.x_ref, f32[16,512]{1,0:T(8,128)} %reshape.154.mass_ref), custom_call_target="tpu_custom_call" | custom-call | tf_op jit(solution)/shard_map/pallas_call | solution.py:159
  58.0 2.3 convolution_bitcast_fusion.3
  60.3 3.2 fusion.36
  65.5 38.1 %shard_map.75 = f32[16,64,128]{2,1,0:T(8,128)} custom-call(f32[16,64,128]{2,1,0:T(8,128)} %reshape.156.x_ref, f32[64,128]{1,0:T(8,128)} %broadcast_in_dim.48.icol_ref), custom_call_target="tpu_custom_call" | custom-call | tf_op jit(solution)/shard_map/pallas_call | solution.py:323
  107.2 2.9 fusion.23
  110.0 3.1 fusion.12
  114.1 13.4 %shard_map.76 = bf16[128,512]{1,0:T(8,128)(2,1)} custom-call(f32[128,512]{1,0:T(8,128)} %reshape.159.x_ref, f32[16,512]{1,0:T(8,128)} %reshape.154.mass_ref), custom_call_target="tpu_custom_call" | custom-call | tf_op jit(solution)/shard_map/pallas_call | solution.py:159
  133.2 3.2 fusion.39
  138.5 37.0 %shard_map.77 = f32[16,64,128]{2,1,0:T(8,128)} custom-call(f32[16,64,128]{2,1,0:T(8,128)} %reshape.161.x_ref, f32[64,128]{1,0:T(8,128)} %broadcast_in_dim.48.icol_ref), custom_call_target="tpu_custom_call" | custom-call | tf_op jit(solution)/shard_map/pallas_call | solution.py:323
  179.0 2.9 fusion.20
  181.9 3.1 fusion.10
  186.0 13.4 %shard_map.78 = bf16[128,512]{1,0:T(8,128)(2,1)} custom-call(f32[128,512]{1,0:T(8,128)} %reshape.163.x_ref, f32[16,512]{1,0:T(8,128)} %reshape.154.mass_ref), custom_call_target="tpu_custom_call" | custom-call | tf_op jit(solution)/shard_map/pallas_call | solution.py:159
  202.7 2.3 convolution_bitcast_fusion.1
  205.1 3.2 fusion.42
  210.4 36.9 %shard_map.79 = f32[16,64,128]{2,1,0:T(8,128)} custom-call(f32[16,64,128]{2,1,0:T(8,128)} %reshape.165.x_ref, f32[64,128]{1,0:T(8,128)} %broadcast_in_dim.48.icol_ref), custom_call_target="tpu_custom_call" | custom-call | tf_op jit(solution)/shard_map/pallas_call | solution.py:323
  250.8 2.9 fusion.17
  253.7 3.1 fusion.8
  257.8 13.0 %shard_map.80 = bf16[128,512]{1,0:T(8,128)(2,1)} custom-call(f32[128,512]{1,0:T(8,128)} %reshape.167.x_ref, f32[16,512]{1,0:T(8,128)} %reshape.154.mass_ref), custom_call_target="tpu_custom_call" | custom-call | tf_op jit(solution)/shard_map/pallas_call | solution.py:159
  276.4 3.2 fusion.45
  281.8 37.5 %shard_map.81 = f32[16,64,128]{2,1,0:T(8,128)} custom-call(f32[16,64,128]{2,1,0:T(8,128)} %reshape.169.x_ref, f32[64,128]{1,0:T(8,128)} %broadcast_in_dim.48.icol_ref), custom_call_target="tpu_custom_call" | custom-call | tf_op jit(solution)/shard_map/pallas_call | solution.py:323
  (66 shorter events, 55.5 us)
Async XLA Ops:
  0.0 23.8 %copy-start = (bf16[1,1,128,4096]{3,2,1,0:T(8,128)(2,1)S(1)}, bf16[1,1,128,4096]{3,2,1,0:T(8,128)(2,1)}, u32[]{:S(2)}) copy-start(bf16[1,1,128,4096]{3,2,1,0:T(8,128)(2,1)} %param.13) | copy-start | bytes 3145732

commit v3 on v2

--- a/solution.py
+++ b/solution.py
@@ -246,11 +246,11 @@
         m, x = carry
         col = jnp.sum(jnp.where(c == j, m, 0.0), axis=1, keepdims=True)
         row = jnp.sum(jnp.where(r == j, m, 0.0), axis=0, keepdims=True)
-        piv = jnp.sqrt(jnp.sum(jnp.where(r1 == j, col, 0.0), axis=0, keepdims=True))
-        lcol = jnp.where(r1 >= j, col / piv, 0.0)
-        lrow = jnp.where(c1 >= j, row / piv, 0.0)
+        inv = 1.0 / jnp.sqrt(jnp.sum(jnp.where(c1 == j, row, 0.0), axis=1, keepdims=True))
+        lcol = jnp.where(r1 >= j, col * inv, 0.0)
+        lrow = jnp.where(c1 >= j, row * inv, 0.0)
         m = m - lcol * lrow
-        xrow = jnp.sum(jnp.where(r == j, x, 0.0), axis=0, keepdims=True) / piv
+        xrow = jnp.sum(jnp.where(r == j, x, 0.0), axis=0, keepdims=True) * inv
         x = jnp.where(r == j, xrow, x)
         x = x - jnp.where(r1 > j, lcol, 0.0) * xrow
         return m, x

time: 325 us -> 325 us (level)
  no operation moved by 1% of the time
where the time goes in v3:
time: 325 us; the launch traced here: 321 us
  Pallas kernels  219 us (67%)
  local copies, waits for them, and re-layouts  48.6 us (15%)
  matrix products  45.9 us (14%)
  other arithmetic  6.31 us (2%)
    pallas_call x4, Pallas kernels, backward_reduce(): pl.pallas_call(functools.partial(_backward_kernel, n, m, scale), out_shap...  150 us
    pallas_call x4, Pallas kernels, forward_reduce(): pl.pallas_call(functools.partial(_forward_kernel, n, ch), out_shape=jax.S...  56.1 us
    pallas_call x1, Pallas kernels, all_gather2(): pl.pallas_call(functools.partial(_gather2_kernel, axis, other, n), out_sh...  13.3 us
    dot_general x4, matrix products, per_device(): jnp.einsum('pbs,skj->pkbj', bwd_hot.reshape(pairs, 2, n_cap), product, pr...  12.7 us
    dot_general x4, matrix products, per_device(): jnp.einsum('rs,ski->rki', fwd_hot, forward_product, precision=lax.Precisi...  12.3 us
    dot_general x4, matrix products, per_device(): jnp.einsum('bij,bkj->bki', square, forward_taken, preferred_element_type=...  11.4 us
    dot_general x4, matrix products, per_device(): jnp.einsum('bij,bki->bkj', square, taken, preferred_element_type=jnp.floa...  9.37 us
    gather x4, local copies, waits for them, and re-layouts, per_device(): taken = jnp.take(weighted, rows_idx, axis=0)  8.62 us

profile of v3, /device:TPU:1, one launch (start us, length us, event | category | flops | bytes accessed | tf_op | source)
XLA Modules:
  0.0 321.2 jit_solution(6010043625096311146)
XLA Ops:
  8.4 13.3 %shard_map.73 = (bf16[256,512]{1,0:T(8,128)(2,1)}, f32[128,128]{1,0:T(8,128)}) custom-call(bf16[16,512]{1,0:T(8,128)(2,1)} %multiply_convert_fusion.3.x_ref, f32[8,128]{1,0:T(8,128)} %scatter.4.y_ref), custom_call_target="tpu_custom_call" | custom-call | tf_op jit(solution)/shard_map/pallas_call | solution.py:210
  25.1 4.1 %copy.28 = bf16[128,64,64]{2,1,0:T(8,128)(2,1)S(1)} copy(bf16[128,64,64]{0,2,1:T(8,128)(2,1)} %bitcast.63) | data formatting | bytes 2097152 | tf_op jit(solution)/shard_map/reshape;squeeze | solution.py:425
  31.4 2.9 fusion.26
  34.3 3.1 fusion.14
  38.4 16.3 %shard_map.74 = bf16[128,512]{1,0:T(8,128)(2,1)} custom-call(f32[128,512]{1,0:T(8,128)} %reshape.153.x_ref, f32[16,512]{1,0:T(8,128)} %reshape.154.mass_ref), custom_call_target="tpu_custom_call" | custom-call | tf_op jit(solution)/shard_map/pallas_call | solution.py:159
  58.0 2.3 convolution_bitcast_fusion.3
  60.3 3.2 fusion.36
  65.5 38.1 %shard_map.75 = f32[16,64,128]{2,1,0:T(8,128)} custom-call(f32[16,64,128]{2,1,0:T(8,128)} %reshape.156.x_ref, f32[64,128]{1,0:T(8,128)} %broadcast_in_dim.48.icol_ref), custom_call_target="tpu_custom_call" | custom-call | tf_op jit(solution)/shard_map/pallas_call | solution.py:323
  107.2 2.9 fusion.23
  110.0 3.1 fusion.12
  114.1 13.4 %shard_map.76 = bf16[128,512]{1,0:T(8,128)(2,1)} custom-call(f32[128,512]{1,0:T(8,128)} %reshape.159.x_ref, f32[16,512]{1,0:T(8,128)} %reshape.154.mass_ref), custom_call_target="tpu_custom_call" | custom-call | tf_op jit(solution)/shard_map/pallas_call | solution.py:159
  133.2 3.2 fusion.39
  138.5 37.0 %shard_map.77 = f32[16,64,128]{2,1,0:T(8,128)} custom-call(f32[16,64,128]{2,1,0:T(8,128)} %reshape.161.x_ref, f32[64,128]{1,0:T(8,128)} %broadcast_in_dim.48.icol_ref), custom_call_target="tpu_custom_call" | custom-call | tf_op jit(solution)/shard_map/pallas_call | solution.py:323
  179.0 2.9 fusion.20
  181.9 3.1 fusion.10
  186.0 13.4 %shard_map.78 = bf16[128,512]{1,0:T(8,128)(2,1)} custom-call(f32[128,512]{1,0:T(8,128)} %reshape.163.x_ref, f32[16,512]{1,0:T(8,128)} %reshape.154.mass_ref), custom_call_target="tpu_custom_call" | custom-call | tf_op jit(solution)/shard_map/pallas_call | solution.py:159
  205.1 3.2 fusion.42
  210.4 36.9 %shard_map.79 = f32[16,64,128]{2,1,0:T(8,128)} custom-call(f32[16,64,128]{2,1,0:T(8,128)} %reshape.165.x_ref, f32[64,128]{1,0:T(8,128)} %broadcast_in_dim.48.icol_ref), custom_call_target="tpu_custom_call" | custom-call | tf_op jit(solution)/shard_map/pallas_call | solution.py:323
  250.8 2.9 fusion.17
  253.7 3.1 fusion.8
  257.8 13.0 %shard_map.80 = bf16[128,512]{1,0:T(8,128)(2,1)} custom-call(f32[128,512]{1,0:T(8,128)} %reshape.167.x_ref, f32[16,512]{1,0:T(8,128)} %reshape.154.mass_ref), custom_call_target="tpu_custom_call" | custom-call | tf_op jit(solution)/shard_map/pallas_call | solution.py:159
  274.1 2.3 convolution_bitcast_fusion
  276.4 3.2 fusion.45
  281.8 37.5 %shard_map.81 = f32[16,64,128]{2,1,0:T(8,128)} custom-call(f32[16,64,128]{2,1,0:T(8,128)} %reshape.169.x_ref, f32[64,128]{1,0:T(8,128)} %broadcast_in_dim.48.icol_ref), custom_call_target="tpu_custom_call" | custom-call | tf_op jit(solution)/shard_map/pallas_call | solution.py:323
  (66 shorter events, 55.5 us)
Async XLA Ops:
  0.0 23.8 %copy-start = (bf16[1,1,128,4096]{3,2,1,0:T(8,128)(2,1)S(1)}, bf16[1,1,128,4096]{3,2,1,0:T(8,128)(2,1)}, u32[]{:S(2)}) copy-start(bf16[1,1,128,4096]{3,2,1,0:T(8,128)(2,1)} %param.13) | copy-start | bytes 3145732

commit v4 on v2

--- a/solution.py
+++ b/solution.py
@@ -259,7 +259,7 @@
     return x
 
 
-def _backward_kernel(n, m, scale, x_ref, icol_ref, o_ref, recv, gath, g3, s1, r1, s2, r2, s3, r3):
+def _backward_kernel(n, m, scale, x_ref, icol_ref, o_ref, recv, gath, gp, g3, s1, r1, s2, r2, s3, r3, s4, r4):
     me = lax.axis_index("row")
     mc = lax.axis_index("col")
     barrier = pltpu.get_barrier_semaphore()
@@ -282,6 +282,15 @@
         c.wait()
         acc = acc + recv[d]
     gath[0] = acc * icol_ref[...]
+    gp[0] = _gram_of(gath[0])
+    grams = []
+    for d in range(1, n):
+        c = pltpu.make_async_remote_copy(
+            gp.at[0], gp.at[d], s4.at[d], r4.at[d],
+            device_id=((me + d) % n, mc), device_id_type=MESH_ID,
+        )
+        c.start()
+        grams.append(c)
     gathers = []
     for d in range(1, n):
         c = pltpu.make_async_remote_copy(
@@ -290,27 +299,28 @@
         )
         c.start()
         gathers.append(c)
-    for c in gathers:
-        c.wait()
-    g = None
-    for p in range(n):
-        term = _gram_of(gath[(me - p + n) % n])
-        g = term if g is None else g + term
+    for c in grams:
+        c.wait()
+    g = gp[me % n]
+    for p in range(1, n):
+        g = g + gp[(me - p + n) % n]
     g3[0] = g
-    grams = []
+    cols = []
     for d in range(1, m):
         c = pltpu.make_async_remote_copy(
             g3.at[0], g3.at[d], s3.at[d], r3.at[d],
             device_id=(me, (mc + d) % m), device_id_type=MESH_ID,
         )
         c.start()
-        grams.append(c)
-    for c in grams:
+        cols.append(c)
+    for c in cols:
         c.wait()
     total = g3[mc % m]
     for q in range(1, m):
         total = total + g3[(mc - q + m) % m]
     inverse = chol_inverse(total * scale)
+    for c in gathers:
+        c.wait()
     for p in range(n):
         o_ref[p] = lax.dot_general(
             inverse, gath[(me - p + n) % n], (((1,), (0,)), ((), ())),
@@ -328,6 +338,7 @@
         scratch_shapes=[
             pltpu.VMEM((n, vecs, lanes), jnp.float32),
             pltpu.VMEM((n, vecs, lanes), jnp.float32),
+            pltpu.VMEM((n, vecs, vecs), jnp.float32),
             pltpu.VMEM((m, vecs, vecs), jnp.float32),
             pltpu.SemaphoreType.DMA((n,)),
             pltpu.SemaphoreType.DMA((n,)),
@@ -335,6 +346,8 @@
             pltpu.SemaphoreType.DMA((n,)),
             pltpu.SemaphoreType.DMA((m,)),
             pltpu.SemaphoreType.DMA((m,)),
+            pltpu.SemaphoreType.DMA((n,)),
+            pltpu.SemaphoreType.DMA((n,)),
         ],
         compiler_params=pltpu.CompilerParams(collective_id=collective_id, has_side_effects=True),
     )(x, icol)

time: 325 us -> 333 us (1.025)
  Pallas kernels: 219 us -> 228 us
    pallas_call x4, Pallas kernels: 150 us -> 160 us  [backward_reduce(): pl.pallas_call(functools.partial(_backward_kernel, n, m, scale), out_shap...]
where the time goes in v4:
time: 333 us; the launch traced here: 330 us
  Pallas kernels  228 us (68%)
  local copies, waits for them, and re-layouts  48.4 us (15%)
  matrix products  45.9 us (14%)
  other arithmetic  6.31 us (2%)
    pallas_call x4, Pallas kernels, backward_reduce(): pl.pallas_call(functools.partial(_backward_kernel, n, m, scale), out_shap...  160 us
    pallas_call x4, Pallas kernels, forward_reduce(): pl.pallas_call(functools.partial(_forward_kernel, n, ch), out_shape=jax.S...  54.8 us
    pallas_call x1, Pallas kernels, all_gather2(): pl.pallas_call(functools.partial(_gather2_kernel, axis, other, n), out_sh...  13.3 us
    dot_general x4, matrix products, per_device(): jnp.einsum('pbs,skj->pkbj', bwd_hot.reshape(pairs, 2, n_cap), product, pr...  12.7 us
    dot_general x4, matrix products, per_device(): jnp.einsum('rs,ski->rki', fwd_hot, forward_product, precision=lax.Precisi...  12.3 us
    dot_general x4, matrix products, per_device(): jnp.einsum('bij,bkj->bki', square, forward_taken, preferred_element_type=...  11.4 us
    dot_general x4, matrix products, per_device(): jnp.einsum('bij,bki->bkj', square, taken, preferred_element_type=jnp.floa...  9.37 us
    gather x4, local copies, waits for them, and re-layouts, per_device(): taken = jnp.take(weighted, rows_idx, axis=0)  8.62 us

profile of v4, /device:TPU:1, one launch (start us, length us, event | category | flops | bytes accessed | tf_op | source)
XLA Modules:
  0.0 329.5 jit_solution(13334905079344406164)
XLA Ops:
  8.4 13.3 %shard_map.73 = (bf16[256,512]{1,0:T(8,128)(2,1)}, f32[128,128]{1,0:T(8,128)}) custom-call(bf16[16,512]{1,0:T(8,128)(2,1)} %multiply_convert_fusion.3.x_ref, f32[8,128]{1,0:T(8,128)} %scatter.4.y_ref), custom_call_target="tpu_custom_call" | custom-call | tf_op jit(solution)/shard_map/pallas_call | solution.py:210
  25.1 4.1 %copy.28 = bf16[128,64,64]{2,1,0:T(8,128)(2,1)S(1)} copy(bf16[128,64,64]{0,2,1:T(8,128)(2,1)} %bitcast.63) | data formatting | bytes 2097152 | tf_op jit(solution)/shard_map/reshape;squeeze | solution.py:438
  31.4 2.9 fusion.26
  34.3 3.1 fusion.14
  38.4 16.3 %shard_map.74 = bf16[128,512]{1,0:T(8,128)(2,1)} custom-call(f32[128,512]{1,0:T(8,128)} %reshape.153.x_ref, f32[16,512]{1,0:T(8,128)} %reshape.154.mass_ref), custom_call_target="tpu_custom_call" | custom-call | tf_op jit(solution)/shard_map/pallas_call | solution.py:159
  58.0 2.3 convolution_bitcast_fusion.3
  60.3 3.2 fusion.36
  65.5 39.6 %shard_map.75 = f32[16,64,128]{2,1,0:T(8,128)} custom-call(f32[16,64,128]{2,1,0:T(8,128)} %reshape.156.x_ref, f32[64,128]{1,0:T(8,128)} %broadcast_in_dim.48.icol_ref), custom_call_target="tpu_custom_call" | custom-call | tf_op jit(solution)/shard_map/pallas_call | solution.py:333
  108.6 2.9 fusion.23
  111.5 3.1 fusion.12
  115.6 13.1 %shard_map.76 = bf16[128,512]{1,0:T(8,128)(2,1)} custom-call(f32[128,512]{1,0:T(8,128)} %reshape.159.x_ref, f32[16,512]{1,0:T(8,128)} %reshape.154.mass_ref), custom_call_target="tpu_custom_call" | custom-call | tf_op jit(solution)/shard_map/pallas_call | solution.py:159
  134.3 3.2 fusion.39
  139.6 40.7 %shard_map.77 = f32[16,64,128]{2,1,0:T(8,128)} custom-call(f32[16,64,128]{2,1,0:T(8,128)} %reshape.161.x_ref, f32[64,128]{1,0:T(8,128)} %broadcast_in_dim.48.icol_ref), custom_call_target="tpu_custom_call" | custom-call | tf_op jit(solution)/shard_map/pallas_call | solution.py:333
  183.9 2.9 fusion.20
  186.8 3.1 fusion.10
  190.9 13.1 %shard_map.78 = bf16[128,512]{1,0:T(8,128)(2,1)} custom-call(f32[128,512]{1,0:T(8,128)} %reshape.163.x_ref, f32[16,512]{1,0:T(8,128)} %reshape.154.mass_ref), custom_call_target="tpu_custom_call" | custom-call | tf_op jit(solution)/shard_map/pallas_call | solution.py:159
  209.7 3.2 fusion.42
  215.0 40.4 %shard_map.79 = f32[16,64,128]{2,1,0:T(8,128)} custom-call(f32[16,64,128]{2,1,0:T(8,128)} %reshape.165.x_ref, f32[64,128]{1,0:T(8,128)} %broadcast_in_dim.48.icol_ref), custom_call_target="tpu_custom_call" | custom-call | tf_op jit(solution)/shard_map/pallas_call | solution.py:333
  258.9 2.9 fusion.17
  261.8 3.1 fusion.8
  265.9 12.3 %shard_map.80 = bf16[128,512]{1,0:T(8,128)(2,1)} custom-call(f32[128,512]{1,0:T(8,128)} %reshape.167.x_ref, f32[16,512]{1,0:T(8,128)} %reshape.154.mass_ref), custom_call_target="tpu_custom_call" | custom-call | tf_op jit(solution)/shard_map/pallas_call | solution.py:159
  281.4 2.3 convolution_bitcast_fusion
  283.8 3.2 fusion.45
  288.9 38.8 %shard_map.81 = f32[16,64,128]{2,1,0:T(8,128)} custom-call(f32[16,64,128]{2,1,0:T(8,128)} %reshape.169.x_ref, f32[64,128]{1,0:T(8,128)} %broadcast_in_dim.48.icol_ref), custom_call_target="tpu_custom_call" | custom-call | tf_op jit(solution)/shard_map/pallas_call | solution.py:333
  (66 shorter events, 55.3 us)
Async XLA Ops:
  0.0 23.8 %copy-start = (bf16[1,1,128,4096]{3,2,1,0:T(8,128)(2,1)S(1)}, bf16[1,1,128,4096]{3,2,1,0:T(8,128)(2,1)}, u32[]{:S(2)}) copy-start(bf16[1,1,128,4096]{3,2,1,0:T(8,128)(2,1)} %param.13) | copy-start | bytes 3145732

commit v5 on v2

--- a/solution.py
+++ b/solution.py
@@ -437,12 +437,8 @@
     row_mass_spread = jnp.broadcast_to(row_mass[:, None, :], (own, vecs, bsize)).reshape(vec_rows, LANES)
     fwd_hot = (fwd_ids[None, :] == jnp.arange(row_panel)[:, None]).astype(jnp.float32)
     bwd_hot = (bwd_ids[None, :] == jnp.arange(col_panel)[:, None]).astype(jnp.float32)
-    for step in range(ITERS):
-        if step == 0:
-            scaled = first_panel
-        else:
-            paired = (current * inv_pairs).astype(jnp.bfloat16)
-            scaled = paired.reshape(pairs, vecs, 2, bsize).transpose(0, 2, 1, 3).reshape(col_panel, vecs, bsize)
+    def iteration(step, carry):
+        scaled, unused = carry
         forward_taken = jnp.take(scaled, cols_idx, axis=0)
         forward_product = jnp.einsum(
             "bij,bkj->bki", square, forward_taken, preferred_element_type=jnp.float32
@@ -460,6 +456,12 @@
             precision=lax.Precision.HIGH, preferred_element_type=jnp.float32,
         ).reshape(pairs, vecs, 2 * bsize)
         current = backward_reduce(summed, own_pair, n_row, n_col, 1.0 / total_boxes, 2)
+        paired = (current * inv_pairs).astype(jnp.bfloat16)
+        scaled = paired.reshape(pairs, vecs, 2, bsize).transpose(0, 2, 1, 3).reshape(col_panel, vecs, bsize)
+        return scaled, current
+
+    start = jnp.zeros((pairs, vecs, 2 * bsize), jnp.float32)
+    unused, current = lax.fori_loop(0, ITERS, iteration, (first_panel, start))
     me = lax.axis_index("row")
     mine = lax.dynamic_index_in_dim(current, me, 0, keepdims=False)
     return mine.reshape(vecs, own, bsize).transpose(1, 0, 2).reshape(own, vecs * bsize)

time: 325 us -> 331 us (1.018)
  local copies, waits for them, and re-layouts: 48.6 us -> 62.9 us
  other arithmetic: 6.31 us -> 2.16 us
  Pallas kernels: 219 us -> 215 us
    unnamed x3 -> x8, local copies, waits for them, and re-layouts: 1.31 us -> 6.23 us
    reshape x12, local copies, waits for them, and re-layouts: 14 us -> 18.5 us  [the longest x4 10.6 us: iteration(): summed = jnp.einsum('pbs,skj->pkbj', bwd_hot.reshape(pairs, 2, n_cap), pr...]
    another operation x5, local copies, waits for them, and re-layouts: 5.29 us -> 1.31 us  [the longest x1 4.11 us: per_device(): square = tile.reshape(n_cap, bsize, bsize)]
    transpose x4, local copies, waits for them, and re-layouts: 2.16 us -> 6.01 us  [iteration(): jnp.einsum('pbs,skj->pkbj', bwd_hot.reshape(pairs, 2, n_cap), product, pr...]
    pallas_call x4, Pallas kernels: 150 us -> 146 us  [backward_reduce(): pl.pallas_call(functools.partial(_backward_kernel, n, m, scale), out_shap...]
where the time goes in v5:
time: 331 us; the launch traced here: 330 us
  Pallas kernels  215 us (65%)
  local copies, waits for them, and re-layouts  62.9 us (19%)
  matrix products  47.9 us (14%)
    pallas_call x4, Pallas kernels, backward_reduce(): pl.pallas_call(functools.partial(_backward_kernel, n, m, scale), out_shap...  146 us
    pallas_call x4, Pallas kernels, forward_reduce(): pl.pallas_call(functools.partial(_forward_kernel, n, ch), out_shape=jax.S...  56.2 us
    dot_general x4, matrix products, iteration(): jnp.einsum('pbs,skj->pkbj', bwd_hot.reshape(pairs, 2, n_cap), product, pr...  13.8 us
    dot_general x4, matrix products, iteration(): jnp.einsum('rs,ski->rki', fwd_hot, forward_product, precision=lax.Precisi...  13.3 us
    pallas_call x1, Pallas kernels, all_gather2(): pl.pallas_call(functools.partial(_gather2_kernel, axis, other, n), out_sh...  13.3 us
    dot_general x4, matrix products, iteration(): jnp.einsum('bij,bkj->bki', square, forward_taken, preferred_element_type=...  11.4 us
    reshape x4, local copies, waits for them, and re-layouts, iteration(): summed = jnp.einsum('pbs,skj->pkbj', bwd_hot.reshape(pairs, 2, n_cap), pr...  10.6 us
    dot_general x4, matrix products, iteration(): jnp.einsum('bij,bki->bkj', square, taken, preferred_element_type=jnp.floa...  9.36 us

profile of v5, /device:TPU:1, one launch (start us, length us, event | category | flops | bytes accessed | tf_op | source)
XLA Modules:
  0.0 329.7 jit_solution(9320641455691913310)
XLA Ops:
  3.5 13.3 %shard_map.73 = (bf16[256,512]{1,0:T(8,128)(2,1)}, f32[128,128]{1,0:T(8,128)}) custom-call(bf16[16,512]{1,0:T(8,128)(2,1)} %multiply_convert_fusion.1.x_ref, f32[8,128]{1,0:T(8,128)} %scatter.4.y_ref), custom_call_target="tpu_custom_call" | custom-call | tf_op jit(solution)/shard_map/pallas_call | solution.py:210
  22.6 4.0 %copy.24 = bf16[128,64,64]{2,1,0:T(8,128)(2,1)S(1)} copy(bf16[128,64,64]{0,2,1:T(8,128)(2,1)} %bitcast.60) | data formatting | bytes 2097152
  26.7 301.4 %while.14 = (s32[]{:T(128)}, bf16[32,64,64]{2,1,0:T(8,128)(2,1)S(1)}, f32[16,64,128]{2,1,0:T(8,128)}, s32[128]{0:T(128)S(1)}, s32[128]{0:T(128)S(1)}, /*index=5*...) while((s32[]{:T(128)}, ...), condition=%wide.region_1.2_spmd.clone, body=%wide.region_0.1_spmd.clone.sunk | while | flops 287064320 | bytes 25091728 | solution.py:464
  29.0 2.9 fusion.61
  31.9 3.3 %fusion.62 = f32[16,64,64]{2,0,1:T(8,128)S(1)} fusion(f32[128,64,64]{2,1,0:T(8,128)S(1)} %fusion.61, s32[128]{0:T(128)S(1)} %get-tuple-element.268), kind=kOutput, calls=%fused_computation.17.clone.1 | convolution fusion | flops 50335744 | bytes 2359808 | tf_op jit(solution)/shard_map/while/body/eval_jaxpr/rs,ski->rki/dot_general | solution.py:446
  37.0 16.3 %eval_jaxpr.2 = bf16[128,512]{1,0:T(8,128)(2,1)} custom-call(f32[128,512]{1,0:T(8,128)} %reshape.185.x_ref, f32[16,512]{1,0:T(8,128)} %reshape.186.mass_ref), custom_call_target="tpu_custom_call" | custom-call | tf_op jit(solution)/shard_map/while/body/eval_jaxpr/pallas_call | solution.py:159
  59.0 3.4 %fusion.64 = f32[16,64,2,64]{3,0,2,1:T(8,128)S(1)} fusion(f32[128,64,64,1]{2,1,0,3:T(8,128)S(1)} %convolution_bitcast_fusion.2, f32[16,2,128]{2,1,0:T(2,128)S(1)} %bitcast.61), kind=kOutput, calls=%fused_computation.16.clone.1 | convolution fusion | flops 100663296 | bytes 2637824 | tf_op jit(solution)/shard_map/while/body/eval_jaxpr/pbs,skj->pkbj/dot_general | solution.py:454
  63.9 2.7 reshape.188.x_ref
  67.2 36.9 %eval_jaxpr.3 = f32[16,64,128]{2,1,0:T(8,128)S(1)} custom-call(f32[16,64,128]{2,1,0:T(8,128)} %reshape.188.x_ref, f32[64,128]{1,0:T(8,128)} %broadcast_in_dim.93.icol_ref), custom_call_target="tpu_custom_call" | custom-call | tf_op jit(solution)/shard_map/while/body/eval_jaxpr/pallas_call | solution.py:323
  107.1 2.9 fusion.61
  110.0 3.3 %fusion.62 = f32[16,64,64]{2,0,1:T(8,128)S(1)} fusion(f32[128,64,64]{2,1,0:T(8,128)S(1)} %fusion.61, s32[128]{0:T(128)S(1)} %get-tuple-element.268), kind=kOutput, calls=%fused_computation.17.clone.1 | convolution fusion | flops 50335744 | bytes 2359808 | tf_op jit(solution)/shard_map/while/body/eval_jaxpr/rs,ski->rki/dot_general | solution.py:446
  115.1 13.4 %eval_jaxpr.2 = bf16[128,512]{1,0:T(8,128)(2,1)} custom-call(f32[128,512]{1,0:T(8,128)} %reshape.185.x_ref, f32[16,512]{1,0:T(8,128)} %reshape.186.mass_ref), custom_call_target="tpu_custom_call" | custom-call | tf_op jit(solution)/shard_map/while/body/eval_jaxpr/pallas_call | solution.py:159
  134.1 3.4 %fusion.64 = f32[16,64,2,64]{3,0,2,1:T(8,128)S(1)} fusion(f32[128,64,64,1]{2,1,0,3:T(8,128)S(1)} %convolution_bitcast_fusion.2, f32[16,2,128]{2,1,0:T(2,128)S(1)} %bitcast.61), kind=kOutput, calls=%fused_computation.16.clone.1 | convolution fusion | flops 100663296 | bytes 2637824 | tf_op jit(solution)/shard_map/while/body/eval_jaxpr/pbs,skj->pkbj/dot_general | solution.py:454
  142.3 36.2 %eval_jaxpr.3 = f32[16,64,128]{2,1,0:T(8,128)S(1)} custom-call(f32[16,64,128]{2,1,0:T(8,128)} %reshape.188.x_ref, f32[64,128]{1,0:T(8,128)} %broadcast_in_dim.93.icol_ref), custom_call_target="tpu_custom_call" | custom-call | tf_op jit(solution)/shard_map/while/body/eval_jaxpr/pallas_call | solution.py:323
  181.5 2.9 fusion.61
  184.4 3.3 %fusion.62 = f32[16,64,64]{2,0,1:T(8,128)S(1)} fusion(f32[128,64,64]{2,1,0:T(8,128)S(1)} %fusion.61, s32[128]{0:T(128)S(1)} %get-tuple-element.268), kind=kOutput, calls=%fused_computation.17.clone.1 | convolution fusion | flops 50335744 | bytes 2359808 | tf_op jit(solution)/shard_map/while/body/eval_jaxpr/rs,ski->rki/dot_general | solution.py:446
  189.4 13.5 %eval_jaxpr.2 = bf16[128,512]{1,0:T(8,128)(2,1)} custom-call(f32[128,512]{1,0:T(8,128)} %reshape.185.x_ref, f32[16,512]{1,0:T(8,128)} %reshape.186.mass_ref), custom_call_target="tpu_custom_call" | custom-call | tf_op jit(solution)/shard_map/while/body/eval_jaxpr/pallas_call | solution.py:159
  208.6 3.4 %fusion.64 = f32[16,64,2,64]{3,0,2,1:T(8,128)S(1)} fusion(f32[128,64,64,1]{2,1,0,3:T(8,128)S(1)} %convolution_bitcast_fusion.2, f32[16,2,128]{2,1,0:T(2,128)S(1)} %bitcast.61), kind=kOutput, calls=%fused_computation.16.clone.1 | convolution fusion | flops 100663296 | bytes 2637824 | tf_op jit(solution)/shard_map/while/body/eval_jaxpr/pbs,skj->pkbj/dot_general | solution.py:454
  216.8 36.1 %eval_jaxpr.3 = f32[16,64,128]{2,1,0:T(8,128)S(1)} custom-call(f32[16,64,128]{2,1,0:T(8,128)} %reshape.188.x_ref, f32[64,128]{1,0:T(8,128)} %broadcast_in_dim.93.icol_ref), custom_call_target="tpu_custom_call" | custom-call | tf_op jit(solution)/shard_map/while/body/eval_jaxpr/pallas_call | solution.py:323
  255.9 2.9 fusion.61
  258.7 3.3 %fusion.62 = f32[16,64,64]{2,0,1:T(8,128)S(1)} fusion(f32[128,64,64]{2,1,0:T(8,128)S(1)} %fusion.61, s32[128]{0:T(128)S(1)} %get-tuple-element.268), kind=kOutput, calls=%fused_computation.17.clone.1 | convolution fusion | flops 50335744 | bytes 2359808 | tf_op jit(solution)/shard_map/while/body/eval_jaxpr/rs,ski->rki/dot_general | solution.py:446
  263.8 13.0 %eval_jaxpr.2 = bf16[128,512]{1,0:T(8,128)(2,1)} custom-call(f32[128,512]{1,0:T(8,128)} %reshape.185.x_ref, f32[16,512]{1,0:T(8,128)} %reshape.186.mass_ref), custom_call_target="tpu_custom_call" | custom-call | tf_op jit(solution)/shard_map/while/body/eval_jaxpr/pallas_call | solution.py:159
  282.5 3.4 %fusion.64 = f32[16,64,2,64]{3,0,2,1:T(8,128)S(1)} fusion(f32[128,64,64,1]{2,1,0,3:T(8,128)S(1)} %convolution_bitcast_fusion.2, f32[16,2,128]{2,1,0:T(2,128)S(1)} %bitcast.61), kind=kOutput, calls=%fused_computation.16.clone.1 | convolution fusion | flops 100663296 | bytes 2637824 | tf_op jit(solution)/shard_map/while/body/eval_jaxpr/pbs,skj->pkbj/dot_general | solution.py:454
  290.7 36.6 %eval_jaxpr.3 = f32[16,64,128]{2,1,0:T(8,128)S(1)} custom-call(f32[16,64,128]{2,1,0:T(8,128)} %reshape.188.x_ref, f32[64,128]{1,0:T(8,128)} %broadcast_in_dim.93.icol_ref), custom_call_target="tpu_custom_call" | custom-call | tf_op jit(solution)/shard_map/while/body/eval_jaxpr/pallas_call | solution.py:323
  (107 shorter events, 67.8 us)
Async XLA Ops:
  22.6 4.0 %copy-start.1 = (s32[1,1,128]{2,1,0:T(1,128)S(1)}, s32[1,1,128]{2,1,0:T(1,128)}, u32[]{:S(2)}) copy-start(s32[1,1,128]{2,1,0:T(1,128)} %param.12) | copy-start | bytes 1540
  22.6 4.0 %copy-start.2 = (s32[1,1,128]{2,1,0:T(1,128)S(1)}, s32[1,1,128]{2,1,0:T(1,128)}, u32[]{:S(2)}) copy-start(s32[1,1,128]{2,1,0:T(1,128)} %param.13) | copy-start | bytes 1540
  22.6 4.0 %copy-start.3 = (f32[2,64]{1,0:T(2,128)S(1)}, f32[2,64]{1,0:T(2,128)}, u32[]{:S(2)}) copy-start(f32[2,64]{1,0:T(2,128)} %param.16) | copy-start | bytes 1540
  104.1 0.8 copy-start
  178.5 0.8 copy-start
  252.9 0.8 copy-start
  327.3 0.8 copy-start
